TPU v7x, 32 devices: a whole 2x2x4 slice. The times are simulated.
32 devices in a mesh: dp: 16 (over z, x, core), head: 2 (over y).
Axes of the slice: x: 2, y: 2, z: 4, core: 2. Of those that a mesh axis runs over, the one named last changes fastest.
Arguments:
- queries: bfloat16 [4096, 8192], P('dp', 'head'), may hold values from -6 to 6
- keys: bfloat16 [4096, 1024], P('dp', 'head'), may hold values from -6 to 6
- values: bfloat16 [4096, 1024], P('dp', 'head'), may hold values from -6 to 6
- output_grad: bfloat16 [4096, 4096], P('dp', 'head'), may hold values from -6 to 6
- out_weight: bfloat16 [8192, 4096], P(('head', 'dp')), may hold values from -0.0625 to 0.0625
- lengths: int32 [16], replicated, may hold values from 1 to 512, 4096 in all
Outputs:
- layer_out: bfloat16 [4096, 4096], P('dp', 'head')
- query_grad: bfloat16 [4096, 8192], P('dp', 'head')
- key_grad: bfloat16 [4096, 1024], P('dp', 'head')
- value_grad: bfloat16 [4096, 1024], P('dp', 'head')
Inputs may be any that keep to these rules, and one draw needn't show every extreme that they name: Each of the 16 lengths is at least 1 and at most 512, they sum to 4096, and one equals 512.
All inputs are finite; a program needn't handle non-finite values.
Results may differ from a plain program's by a relative error of at most 0.028.
Values may be sent and summed in bfloat16 or wider, within the bound.
A program may use at most 128 MiB of HBM per device.

v0:
```python
import math

import jax
import jax.numpy as jnp
from jax import lax
from jax.sharding import PartitionSpec as P

HD = 128
SPAN = 2


masked_score = -1e30


def passed_along(block, axis, distance):
    devices = range(lax.axis_size(axis))
    route = [(i - distance, i) for i in devices if i - distance in devices]
    return lax.ppermute(block, axis, route)


def doc_start(lengths, positions):
    doc_ends = jnp.cumsum(lengths)
    closed = doc_ends[None, :] <= positions[:, None]
    return jnp.sum(jnp.where(closed, lengths[None, :], 0), axis=1)


def attend(queries, key_rows, value_rows, d_attended, visible, head_dim):
    row_count = queries.shape[0]
    kv_heads = key_rows.shape[1] // head_dim
    group_ratio = queries.shape[1] // key_rows.shape[1]
    scaling = 1.0 / math.sqrt(head_dim)
    grouped = queries.reshape(row_count, kv_heads, group_ratio, head_dim)
    keyed = key_rows.reshape(-1, kv_heads, head_dim)
    valued = value_rows.reshape(-1, kv_heads, head_dim)
    upstream = d_attended.reshape(row_count, kv_heads, group_ratio, head_dim)
    scores = (
        jnp.einsum("tgrd,ngd->grtn", grouped, keyed, preferred_element_type=jnp.float32) * scaling
    )
    scores = jnp.where(visible[None, None], scores, masked_score)
    maximum = jnp.max(scores, axis=-1, keepdims=True)
    weights = jnp.exp(scores - maximum)
    shares = weights / jnp.sum(weights, axis=-1, keepdims=True)
    shares_low = shares.astype(jnp.bfloat16)
    attended = jnp.einsum(
        "grtn,ngd->tgrd", shares_low, valued, preferred_element_type=jnp.float32
    ).astype(jnp.bfloat16)
    row_dots = jnp.sum(upstream.astype(jnp.float32) * attended.astype(jnp.float32), axis=-1)
    d_shares = jnp.einsum("tgrd,ngd->grtn", upstream, valued, preferred_element_type=jnp.float32)
    dscore = (shares * (d_shares - jnp.transpose(row_dots, (1, 2, 0))[..., None]) * scaling).astype(
        jnp.bfloat16
    )
    query_grad = jnp.einsum(
        "grtn,ngd->tgrd", dscore, keyed, preferred_element_type=jnp.float32
    ).astype(jnp.bfloat16)
    key_part = jnp.einsum("grtn,tgrd->ngd", dscore, grouped, preferred_element_type=jnp.float32)
    value_part = jnp.einsum(
        "grtn,tgrd->ngd", shares_low, upstream, preferred_element_type=jnp.float32
    )
    return (
        attended.reshape(row_count, -1),
        query_grad.reshape(row_count, -1),
        key_part.reshape(-1, kv_heads * head_dim),
        value_part.reshape(-1, kv_heads * head_dim),
    )


def on_device(queries, keys, values, output_grad, out_weight, lengths):
    block_rows = queries.shape[0]
    device = lax.axis_index("dp")
    group_weight = lax.all_gather(out_weight, "dp", axis=0, tiled=True)
    upstream_all = lax.all_gather(output_grad, "head", axis=1, tiled=True)
    d_attended = jnp.einsum(
        "tc,rc->tr", upstream_all, group_weight, preferred_element_type=jnp.float32
    ).astype(jnp.bfloat16)
    earlier = [passed_along((keys, values), "dp", offset) for offset in range(1, SPAN + 1)]
    key_rows = jnp.concatenate([couple[0] for couple in earlier[::-1]] + [keys], axis=0)
    value_rows = jnp.concatenate([couple[1] for couple in earlier[::-1]] + [values], axis=0)
    owner_positions = device * block_rows + jnp.arange(block_rows, dtype=jnp.int32)
    owner_starts = doc_start(lengths, owner_positions)
    key_positions = (device - SPAN) * block_rows + jnp.arange(
        (SPAN + 1) * block_rows, dtype=jnp.int32
    )
    visible = (key_positions[None, :] >= owner_starts[:, None]) & (
        key_positions[None, :] <= owner_positions[:, None]
    )
    first_row = 0 * block_rows
    attended, query_grad, key_part, value_part = attend(
        queries, key_rows, value_rows, d_attended, visible, HD
    )
    padding = jnp.zeros((first_row, key_part.shape[1]), jnp.float32)
    attended, query_grad, key_all, value_all = (
        attended,
        query_grad,
        jnp.concatenate([padding, key_part], axis=0),
        jnp.concatenate([padding, value_part], axis=0),
    )
    projected = jnp.dot(attended, group_weight, preferred_element_type=jnp.float32)
    layer_out = lax.psum_scatter(
        projected.astype(jnp.bfloat16), "head", scatter_dimension=1, tiled=True
    )

    def block_of(all_rows, offset):
        return all_rows[(SPAN - offset) * block_rows : (SPAN - offset + 1) * block_rows]

    key_home = block_of(key_all, 0)
    value_home = block_of(value_all, 0)
    for offset in range(1, SPAN + 1):
        returned = (
            passed_along(block_of(key_all, offset).astype(jnp.bfloat16), "dp", -offset).astype(
                jnp.float32
            ),
            passed_along(block_of(value_all, offset).astype(jnp.bfloat16), "dp", -offset).astype(
                jnp.float32
            ),
        )
        key_home = key_home + returned[0]
        value_home = value_home + returned[1]
    return (layer_out, query_grad, key_home.astype(jnp.bfloat16), value_home.astype(jnp.bfloat16))


def solution(mesh):
    return jax.shard_map(
        on_device,
        mesh=mesh,
        in_specs=(
            P("dp", "head"),
            P("dp", "head"),
            P("dp", "head"),
            P("dp", "head"),
            P(("head", "dp"), None),
            P(),
        ),
        out_specs=(P("dp", "head"), P("dp", "head"), P("dp", "head"), P("dp", "head")),
        check_vma=False,
    )
```

profile of v0, /device:TPU:17, one launch (start us, length us, event | category | flops | bytes accessed | tf_op | source)
XLA Modules:
  0.0 331.2 jit_solution(11108983462621138372)
XLA Ops:
  8.7 1.1 copy.53
  9.8 3.1 collective-permute-start.2
  12.9 4.0 %collective-permute-start.3 = (bf16[256,512]{0,1:T(8,128)(2,1)S(1)}, bf16[256,512]{0,1:T(8,128)(2,1)}, u32[]{:S(2)}, u32[]{:S(2)}) collective-permute-start(bf16[256,512]{0,1:T(8,128)(2,1)S(1)} %copy.53), channel_id=1, source_target_pairs={{0,2},{2,4},{4,6},{6,8},{8,10},{10,12},{12,14},{14,16},{16,18},{18... | collective-permute-start | bytes 786440 | tf_op jit(solution)/shard_map/ppermute | solution.py:18
  16.9 3.1 collective-permute-start
  20.1 2.2 collective-permute-start.1
  23.9 3.3 copy.88
  27.2 1.1 compare_and_fusion
  29.1 1.3 collective-permute-done.1
  30.4 0.9 pad_maximum_fusion
  31.3 1.4 copy.51
  32.7 1.9 pad_maximum_fusion.1
  34.7 14.0 %fusion.15 = (f32[4,8,256]{2,1,0:T(8,128)S(1)}, f32[4,8,256,768]{2,3,1,0:T(8,128)}) fusion(pred[256,768]{0,1:T(8,128)(4,1)} %compare_and_fusion, bf16[768,4,128,1]{0,2,3,1:T(8,128)(2,1)} %bitcast.89, bf16[256,4,8,128]{0,3,2,1:T(8,128)(2,1)S(1)} %bitcast.84), kind=kOutput, calls=%fused_computation.33 | convolution fusion | flops 1635779328 | bytes 28278784 | tf_op jit(solution)/shard_map/sub | solution.py:41
  48.7 14.4 %fusion.8 = bf16[4,8,256,768]{2,3,1,0:T(8,128)(2,1)} fusion(f32[4,8,256,768]{2,3,1,0:T(8,128)} %get-tuple-element.21, f32[4,8,256]{2,1,0:T(8,128)S(1)} %get-tuple-element.20), kind=kLoop, calls=%fused_computation.12 | loop fusion | flops 12582912 | bytes 37781504 | tf_op jit(solution)/shard_map/convert_element_type | solution.py:43
  63.1 150.7 %all-gather.3.cloned.1.call-done = bf16[4096,4096]{1,0:T(8,128)(2,1)} async-done(((bf16[256,4096]{1,0:T(8,128)(2,1)}), bf16[4096,4096]{1,0:T(8,128)(2,1)}) %all-gather.3.cloned.1.call-update) | async-done | bytes 33554448 | tf_op jit(solution)/shard_map/all_gather | solution.py:70
  213.8 16.8 %convolution_convert_fusion.1 = bf16[256,4096]{1,0:T(8,128)(2,1)} fusion(bf16[256,4096]{1,0:T(8,128)(2,1)} %all-gather.5.cloned.1.call-done, bf16[4096,4096]{1,0:T(8,128)(2,1)} %all-gather.3.cloned.1.call-done), kind=kOutput, calls=%fused_computation.14 | convolution fusion | flops 8590983168 | bytes 37748736 | tf_op jit(solution)/shard_map/tc,rc->tr/dot_general | solution.py:72
  230.7 3.3 copy.59
  233.9 9.9 %fusion.17 = (bf16[768,4,128]{0,2,1:T(8,128)(2,1)S(1)}, f32[768,4,128]{0,2,1:T(8,128)}) fusion(bf16[256,4,8,128]{0,3,2,1:T(8,128)(2,1)S(1)} %bitcast.81, bf16[4,8,256,768]{2,3,1,0:T(8,128)(2,1)} %fusion.8), kind=kOutput, calls=%fused_computation.35 | convolution fusion | flops 1611005952 | bytes 17039360 | tf_op jit(solution)/shard_map/grtn,tgrd->ngd/dot_general | solution.py:56
  244.7 2.3 collective-permute-start.6
  247.9 2.7 collective-permute-start.7
  250.6 6.4 %multiply_reduce_fusion = (f32[256,4,8]{0,2,1:T(8,128)S(1)}, bf16[4,128,8,256]{3,1,2,0:T(8,128)(2,1)S(1)}) fusion(bf16[256,4096]{0,1:T(8,128)(2,1)S(1)} %copy.59, bf16[768,4,128,1]{0,2,3,1:T(8,128)(2,1)S(1)} %bitcast.87, bf16[4,8,256,768]{2,3,1,0:T(8,128)(2,1)} %fusion.8), kind=kOutput, calls=%fused_computation.15 | convolution fusion | flops 1615847424 | bytes 17596416 | tf_op jit(solution)/shard_map/grtn,ngd->tgrd/dot_general | solution.py:44
  257.0 16.7 %convolution_convert_fusion = bf16[256,4096]{1,0:T(8,128)(2,1)} fusion(bf16[256,4096]{0,1:T(8,128)(2,1)S(1)} %bitcast.83, bf16[4096,4096]{1,0:T(8,128)(2,1)} %all-gather.3.cloned.1.call-done), kind=kOutput, calls=%fused_computation.13 | convolution fusion | flops 8590983168 | bytes 37748736 | tf_op jit(solution)/shard_map/dot_general | solution.py:97
  273.8 15.3 %fusion.3 = bf16[4,8,256,768]{2,3,1,0:T(8,128)(2,1)} fusion(f32[4,8,256]{2,1,0:T(8,128)S(1)} %bitcast.97, f32[4,8,256,768]{2,3,1,0:T(8,128)} %get-tuple-element.21, f32[4,8,256]{2,1,0:T(8,128)S(1)} %get-tuple-element.20, bf16[768,4,128,1]{0,2,3,1:T(8,128)(2,1)S(1)} %bitcast.88, bf16[256,4,8,128]{0,3,2,1:T(8,128)(2,1)S(1)} %bitcast.82), kind=kOutput, calls=%fused_computation.4 | convolution fusion | flops 1642070016 | bytes 40697856 | tf_op jit(solution)/shard_map/tgrd,ngd->grtn/dot_general | solution.py:48
  289.1 10.6 %fusion.16 = (bf16[768,4,128]{0,2,1:T(8,128)(2,1)S(1)}, f32[768,4,128]{0,2,1:T(8,128)}) fusion(bf16[4,8,256,768]{2,3,1,0:T(8,128)(2,1)} %fusion.3, bf16[256,4,8,128]{0,3,2,1:T(8,128)(2,1)} %bitcast.85), kind=kOutput, calls=%fused_computation.34 | convolution fusion | flops 1611005952 | bytes 17039360 | tf_op jit(solution)/shard_map/grtn,tgrd->ngd/dot_general | solution.py:55
  300.6 3.0 collective-permute-start.4
  304.5 2.9 collective-permute-start.5
  307.4 6.4 %convolution_convert_fusion.2 = bf16[4,128,8,256]{3,1,2,0:T(8,128)(2,1)S(1)} fusion(bf16[768,4,128,1]{0,2,3,1:T(8,128)(2,1)S(1)} %bitcast.90, bf16[4,8,256,768]{2,3,1,0:T(8,128)(2,1)} %fusion.3), kind=kOutput, calls=%fused_computation.17 | convolution fusion | flops 1611661312 | bytes 15466496 | tf_op jit(solution)/shard_map/grtn,ngd->tgrd/dot_general | solution.py:52
  313.8 1.1 slice.43
  315.1 1.9 slice.40
  317.0 1.2 copy.66
  318.2 2.9 copy.72
  321.1 1.8 add_convert_fusion
  322.9 1.8 add_convert_fusion.1
  (34 shorter events, 7.6 us)
Async XLA Ops:
  7.2 23.2 %copy-start.2 = (bf16[256,512]{1,0:T(8,128)(2,1)S(1)}, bf16[256,512]{1,0:T(8,128)(2,1)}, u32[]{:S(2)}) copy-start(bf16[256,512]{1,0:T(8,128)(2,1)} %param.8) | copy-start | bytes 786436
  7.2 55.9 %all-gather.5.cloned.1.call-start = ((), (), s32[]{:S(2)}) async-start(), calls=%async_computation.3 | async-start | bytes 3145728 | tf_op jit(solution)/shard_map/all_gather | solution.py:71
  7.9 205.9 %all-gather.3.cloned.1.call-start = ((), (), s32[]{:S(2)}) async-start(), calls=%async_computation.1 | async-start | bytes 35651584 | tf_op jit(solution)/shard_map/all_gather | solution.py:70
  8.7 316.0 %reduce-scatter.2.cloned.1.call-start = ((), (), s32[]{:S(2)}) async-start(), calls=%async_computation.2 | async-start | bytes 3145728 | tf_op jit(solution)/shard_map/reduce_scatter | solution.py:98
  9.8 22.9 %collective-permute-start.2 = (bf16[256,512]{0,1:T(8,128)(2,1)S(1)}, bf16[256,512]{0,1:T(8,128)(2,1)S(1)}, u32[]{:S(2)}, u32[]{:S(2)}) collective-permute-start(bf16[256,512]{0,1:T(8,128)(2,1)S(1)} %copy.53), channel_id=1, source_target_pairs={{0,4},{2,6},{4,8},{6,10},{8,12},{10,14},{12,16},{14,18},{16,20},{1... | collective-permute-start | bytes 786440 | tf_op jit(solution)/shard_map/ppermute | solution.py:18
  12.9 19.8 %collective-permute-start.3 = (bf16[256,512]{0,1:T(8,128)(2,1)S(1)}, bf16[256,512]{0,1:T(8,128)(2,1)}, u32[]{:S(2)}, u32[]{:S(2)}) collective-permute-start(bf16[256,512]{0,1:T(8,128)(2,1)S(1)} %copy.53), channel_id=1, source_target_pairs={{0,2},{2,4},{4,6},{6,8},{8,10},{10,12},{12,14},{14,16},{16,18},{18... | collective-permute-start | bytes 786440 | tf_op jit(solution)/shard_map/ppermute | solution.py:18
  16.9 12.2 %collective-permute-start = (bf16[256,512]{1,0:T(8,128)(2,1)}, bf16[256,512]{1,0:T(8,128)(2,1)S(1)}, u32[]{:S(2)}, u32[]{:S(2)}) collective-permute-start(bf16[256,512]{1,0:T(8,128)(2,1)} %param.8), channel_id=1, source_target_pairs={{0,4},{2,6},{4,8},{6,10},{8,12},{10,14},{12,16},{14,18},{16,20},{1... | collective-permute-start | bytes 786440 | tf_op jit(solution)/shard_map/ppermute | solution.py:18
  20.1 10.3 %collective-permute-start.1 = (bf16[256,512]{1,0:T(8,128)(2,1)}, bf16[256,512]{1,0:T(8,128)(2,1)S(1)}, u32[]{:S(2)}, u32[]{:S(2)}) collective-permute-start(bf16[256,512]{1,0:T(8,128)(2,1)} %param.8), channel_id=1, source_target_pairs={{0,2},{2,4},{4,6},{6,8},{8,10},{10,12},{12,14},{14,16},{16,18},{18... | collective-permute-start | bytes 786440 | tf_op jit(solution)/shard_map/ppermute | solution.py:18
  27.2 21.5 %copy-start = (bf16[256,4096]{0,1:T(8,128)(2,1)}, bf16[256,4096]{0,1:T(8,128)(2,1)S(1)}, u32[]{:S(2)}) copy-start(bf16[256,4096]{0,1:T(8,128)(2,1)S(1)} %copy.88) | copy-start | bytes 6291460
  244.7 76.4 %collective-permute-start.6 = (bf16[256,512]{1,0:T(8,128)(2,1)}, bf16[256,512]{1,0:T(8,128)(2,1)S(1)}, u32[]{:S(2)}, u32[]{:S(2)}) collective-permute-start(bf16[256,512]{1,0:T(8,128)(2,1)} %copy.69), channel_id=1, source_target_pairs={{2,0},{4,2},{6,4},{8,6},{10,8},{12,10},{14,12},{16,14},{18,16},{20... | collective-permute-start | bytes 786440 | tf_op jit(solution)/shard_map/ppermute | solution.py:18
  247.9 73.2 %collective-permute-start.7 = (bf16[256,512]{1,0:T(8,128)(2,1)}, bf16[256,512]{1,0:T(8,128)(2,1)}, u32[]{:S(2)}, u32[]{:S(2)}) collective-permute-start(bf16[256,512]{1,0:T(8,128)(2,1)} %copy.71), channel_id=1, source_target_pairs={{4,0},{6,2},{8,4},{10,6},{12,8},{14,10},{16,12},{18,14},{20,16},{2... | collective-permute-start | bytes 786440 | tf_op jit(solution)/shard_map/ppermute | solution.py:18
  289.1 18.3 %copy-start.1 = (bf16[768,512]{0,1:T(8,128)(2,1)S(1)}, bf16[768,512]{0,1:T(8,128)(2,1)}, u32[]{:S(2)}) copy-start(bf16[768,512]{0,1:T(8,128)(2,1)} %pad_maximum_fusion.1) | copy-start | bytes 2359300
  300.6 22.2 %collective-permute-start.4 = (bf16[256,512]{1,0:T(8,128)(2,1)}, bf16[256,512]{1,0:T(8,128)(2,1)}, u32[]{:S(2)}, u32[]{:S(2)}) collective-permute-start(bf16[256,512]{1,0:T(8,128)(2,1)} %copy.65), channel_id=1, source_target_pairs={{2,0},{4,2},{6,4},{8,6},{10,8},{12,10},{14,12},{16,14},{18,16},{20... | collective-permute-start | bytes 786440 | tf_op jit(solution)/shard_map/ppermute | solution.py:18
  304.5 18.4 %collective-permute-start.5 = (bf16[256,512]{1,0:T(8,128)(2,1)}, bf16[256,512]{1,0:T(8,128)(2,1)}, u32[]{:S(2)}, u32[]{:S(2)}) collective-permute-start(bf16[256,512]{1,0:T(8,128)(2,1)} %copy.67), channel_id=1, source_target_pairs={{4,0},{6,2},{8,4},{10,6},{12,8},{14,10},{16,12},{18,14},{20,16},{2... | collective-permute-start | bytes 786440 | tf_op jit(solution)/shard_map/ppermute | solution.py:18
Sparse Core Ops, SparseCore 0:
  9.5 33.9 all-gather.4
  45.2 168.6 all-gather.2
  273.9 33.3 reduce-scatter.1
where the time goes:
time: 332 us; the launch traced here: 331 us
  waiting for transfers between devices  154 us (46%)
  matrix products  96.2 us (29%)
  starting transfers between devices  23.6 us (7%)
  other arithmetic  22.9 us (7%)
  local copies, waits for them, and re-layouts  20.5 us (6%)
  between operations  13.9 us (4%)
    all_gather x1, waiting for transfers between devices, on_device(): group_weight = lax.all_gather(out_weight, 'dp', axis=0, tiled=True)  151 us
    ppermute x8, starting transfers between devices, passed_along(): return lax.ppermute(block, axis, route)  23.4 us
    dot_general x1, matrix products, on_device(): jnp.einsum('tc,rc->tr', upstream_all, group_weight, preferred_element_typ...  16.8 us
    dot_general x1, matrix products, on_device(): jnp.dot(attended, group_weight, preferred_element_type=jnp.float32)  16.7 us
    dot_general x1, matrix products, attend(): jnp.einsum('tgrd,ngd->grtn', upstream, valued, preferred_element_type=jnp...  15.3 us
    convert_element_type x1, other arithmetic, attend(): shares_low = shares.astype(jnp.bfloat16)  14.4 us
    sub x1, matrix products, attend(): weights = jnp.exp(scores - maximum)  14 us
    dot_general x1, matrix products, attend(): jnp.einsum('grtn,tgrd->ngd', dscore, grouped, preferred_element_type=jnp....  10.6 us
  transfers between devices with their start and end apart: 11, of which 3 were waited for; matrix products, arithmetic and copies ran while one was open for 33% of the time, Pallas kernels for 0%

commit v1 on v0

v1 whole, which is shorter than its diff:
```python
import functools
import math

import jax
import jax.numpy as jnp
from jax import lax
from jax.experimental import pallas as pl
from jax.sharding import PartitionSpec as P

HD = 128
SPAN = 2

masked_score = -1e30


def passed_along(block, axis, distance):
    devices = range(lax.axis_size(axis))
    route = [(i - distance, i) for i in devices if i - distance in devices]
    return lax.ppermute(block, axis, route)


def swapped(block, axis):
    return lax.ppermute(block, axis, [(0, 1), (1, 0)])


def doc_start(lengths, positions):
    doc_ends = jnp.cumsum(lengths)
    closed = doc_ends[None, :] <= positions[:, None]
    return jnp.sum(jnp.where(closed, lengths[None, :], 0), axis=1)


def mm(a, b, contract):
    return lax.dot_general(a, b, ((contract[:1], contract[1:]), ((), ())), preferred_element_type=jnp.float32)


def forward_kernel(chunks, ratio, starts_ref, q_ref, kv_ref, *outs):
    att_refs, shares_ref = outs[:chunks], outs[chunks]
    rows = q_ref.shape[0]
    window = kv_ref.shape[1]
    keys = kv_ref[0]
    values_t = kv_ref[1].T
    key_pos = lax.broadcasted_iota(jnp.int32, (window, rows), 0)
    query_pos = lax.broadcasted_iota(jnp.int32, (window, rows), 1) + (window - rows)
    visible = (key_pos >= starts_ref[...]) & (key_pos <= query_pos)
    scaling = 1.0 / math.sqrt(HD)
    for h in range(ratio):
        c, j = h % chunks, h // chunks
        scores = mm(keys, q_ref[:, h * HD : (h + 1) * HD], (1, 1)) * scaling
        scores = jnp.where(visible, scores, masked_score)
        weights = jnp.exp(scores - jnp.max(scores, axis=0, keepdims=True))
        shares = (weights * (1.0 / jnp.sum(weights, axis=0, keepdims=True))).astype(jnp.bfloat16)
        shares_ref[c, 0, j] = shares
        attended = mm(values_t, shares, (1, 0))
        att_refs[c][:, j * HD : (j + 1) * HD] = attended.T.astype(jnp.bfloat16)


def attend_forward(starts, queries, kv, chunks):
    rows, heads = queries.shape[0], queries.shape[1] // HD
    window, groups = kv.shape[1], kv.shape[2] // HD
    ratio = heads // groups
    per = ratio // chunks
    return pl.pallas_call(
        functools.partial(forward_kernel, chunks, ratio),
        grid=(groups,),
        in_specs=[
            pl.BlockSpec((1, rows), lambda g: (0, 0)),
            pl.BlockSpec((rows, ratio * HD), lambda g: (0, g)),
            pl.BlockSpec((2, window, HD), lambda g: (0, 0, g)),
        ],
        out_specs=[pl.BlockSpec((rows, per * HD), lambda g: (0, g))] * chunks
        + [pl.BlockSpec((chunks, 1, per, window, rows), lambda g: (0, g, 0, 0, 0))],
        out_shape=[jax.ShapeDtypeStruct((rows, heads // chunks * HD), jnp.bfloat16)] * chunks
        + [jax.ShapeDtypeStruct((chunks, groups, per, window, rows), jnp.bfloat16)],
        cost_estimate=pl.CostEstimate(
            flops=8 * heads * rows * window * HD, bytes_accessed=2 * heads * rows * window, transcendentals=heads * rows * window
        ),
        name="attend_forward",
    )(starts, queries, kv)


def backward_kernel(c, chunks, ratio, *refs):
    per = ratio // chunks
    last = c == chunks - 1
    q_ref, kv_ref, shares_ref, da_ref, att_ref = refs[:5]
    earlier = refs[5 : 5 + c + (c > 0)]
    outs = refs[5 + len(earlier) :]
    rows = q_ref.shape[0]
    window = kv_ref.shape[1]
    keys_t = kv_ref[0].T
    values = kv_ref[1]
    scaling = 1.0 / math.sqrt(HD)
    dk = earlier[-1][0] if c > 0 else jnp.zeros((window, HD), jnp.float32)
    dv = earlier[-1][1] if c > 0 else jnp.zeros((window, HD), jnp.float32)
    for j in range(per):
        h = j * chunks + c
        da = da_ref[:, j * HD : (j + 1) * HD]
        att = att_ref[:, j * HD : (j + 1) * HD]
        shares = shares_ref[0, 0, j]
        row_dots = jnp.sum((da.astype(jnp.float32) * att.astype(jnp.float32)).T, axis=0, keepdims=True)
        d_shares = mm(values, da, (1, 1))
        dscore = (shares.astype(jnp.float32) * ((d_shares - row_dots) * scaling)).astype(jnp.bfloat16)
        dq = mm(keys_t, dscore, (1, 0)).T.astype(jnp.bfloat16)
        place = h if last else j
        outs[0][:, place * HD : (place + 1) * HD] = dq
        if last:
            for b in range(c):
                where = j * chunks + b
                outs[0][:, where * HD : (where + 1) * HD] = earlier[b][:, j * HD : (j + 1) * HD]
        dk = dk + mm(dscore, q_ref[:, h * HD : (h + 1) * HD], (1, 0))
        dv = dv + mm(shares, da, (1, 0))
    if last:
        for part, total in ((0, dk), (1, dv)):
            outs[1][part] = total[window - rows :]
            for offset in range(1, SPAN + 1):
                first = window - (offset + 1) * rows
                outs[1 + offset][part] = total[first : first + rows].astype(jnp.bfloat16)
    else:
        outs[1][0] = dk
        outs[1][1] = dv


def attend_backward(c, chunks, queries, kv, shares, d_attended, attended, earlier):
    rows, heads = queries.shape[0], queries.shape[1] // HD
    window, groups = kv.shape[1], kv.shape[2] // HD
    ratio = heads // groups
    per = ratio // chunks
    last = c == chunks - 1
    wide = pl.BlockSpec((rows, ratio * HD), lambda g: (0, g))
    narrow = pl.BlockSpec((rows, per * HD), lambda g: (0, g))
    pair = pl.BlockSpec((2, window, HD), lambda g: (0, 0, g))
    home = pl.BlockSpec((2, rows, HD), lambda g: (0, 0, g))
    if last:
        out_specs = [wide] + [home] * (SPAN + 1)
        out_shape = [
            jax.ShapeDtypeStruct(queries.shape, jnp.bfloat16),
            jax.ShapeDtypeStruct((2, rows, groups * HD), jnp.float32),
        ] + [jax.ShapeDtypeStruct((2, rows, groups * HD), jnp.bfloat16)] * SPAN
    else:
        out_specs = [narrow, pair]
        out_shape = [
            jax.ShapeDtypeStruct((rows, heads // chunks * HD), jnp.bfloat16),
            jax.ShapeDtypeStruct(kv.shape, jnp.float32),
        ]
    return pl.pallas_call(
        functools.partial(backward_kernel, c, chunks, ratio),
        grid=(groups,),
        in_specs=[
            wide,
            pair,
            pl.BlockSpec((1, 1, per, window, rows), lambda g: (c, g, 0, 0, 0)),
            narrow,
            narrow,
        ]
        + ([narrow] * c + [pair] if c > 0 else []),
        out_specs=out_specs,
        out_shape=out_shape,
        cost_estimate=pl.CostEstimate(
            flops=16 * heads // chunks * rows * window * HD,
            bytes_accessed=2 * heads // chunks * rows * window,
            transcendentals=0,
        ),
    )(queries, kv, shares, d_attended, attended, *earlier)


def whole_step(queries, keys, values, output_grad, out_weight, lengths):
    block_rows = queries.shape[0]
    device = lax.axis_index("dp")
    side = lax.axis_index("head")
    two_sided = lax.axis_size("head") == 2
    own_width = output_grad.shape[1]
    ratio = queries.shape[1] // keys.shape[1]
    chunks = out_weight.shape[0] // HD if out_weight.shape[0] % HD == 0 else 1
    if chunks == 0 or ratio % chunks:
        chunks = 1
    depth = out_weight.shape[0] // chunks

    weights = [
        lax.all_gather(out_weight[c * depth : (c + 1) * depth], "dp", axis=0, tiled=True)
        for c in range(chunks)
    ]
    couple = jnp.stack([keys, values])
    earlier = [passed_along(couple, "dp", offset) for offset in range(1, SPAN + 1)]
    kv = jnp.concatenate(earlier[::-1] + [couple], axis=1)
    if two_sided:
        other = swapped(output_grad, "head")
        upstream_all = jnp.where(
            side == 0,
            jnp.concatenate([output_grad, other], axis=1),
            jnp.concatenate([other, output_grad], axis=1),
        )
    else:
        upstream_all = lax.all_gather(output_grad, "head", axis=1, tiled=True)

    positions = device * block_rows + jnp.arange(block_rows, dtype=jnp.int32)
    starts = doc_start(lengths, positions) - (device - SPAN) * block_rows
    *attended, shares = attend_forward(starts[None, :], queries, kv, chunks)

    projected = None
    query_parts, total = [], None
    for c in range(chunks):
        d_attended = mm(upstream_all, weights[c], (1, 1)).astype(jnp.bfloat16)
        part = mm(attended[c], weights[c], (1, 0))
        projected = part if projected is None else projected + part
        if c == chunks - 1:
            if two_sided:
                theirs = lax.dynamic_slice_in_dim(projected, (1 - side) * own_width, own_width, 1)
                ours = lax.dynamic_slice_in_dim(projected, side * own_width, own_width, 1)
            else:
                theirs, ours = projected, projected
            d_attended, theirs = lax.optimization_barrier((d_attended, theirs.astype(jnp.bfloat16)))
        passed = query_parts + [total] if c > 0 else []
        query_grad, *sums = attend_backward(
            c, chunks, queries, kv, shares, d_attended, attended[c], passed
        )
        if c < chunks - 1:
            query_parts.append(query_grad)
            total, projected, upstream_all, attended[c + 1] = lax.optimization_barrier(
                (sums[0], projected, upstream_all, attended[c + 1])
            )

    if two_sided:
        arrived = swapped(theirs, "head")
        layer_out = (ours + arrived.astype(jnp.float32)).astype(jnp.bfloat16)
    else:
        layer_out = lax.psum_scatter(theirs, "head", scatter_dimension=1, tiled=True)
    home = sums[0]
    for offset in range(1, SPAN + 1):
        home = home + passed_along(sums[offset], "dp", -offset).astype(jnp.float32)
    home = home.astype(jnp.bfloat16)
    return layer_out, query_grad, home[0], home[1]


def solution(mesh):
    return jax.shard_map(
        whole_step,
        mesh=mesh,
        in_specs=(
            P("dp", "head"),
            P("dp", "head"),
            P("dp", "head"),
            P("dp", "head"),
            P(("head", "dp"), None),
            P(),
        ),
        out_specs=(P("dp", "head"), P("dp", "head"), P("dp", "head"), P("dp", "head")),
        check_vma=False,
    )
```

time: 332 us -> 352 us (1.060)
  waiting for transfers between devices: 154 us -> 212 us
  matrix products: 96.2 us -> 42.4 us
  Pallas kernels: 0 us -> 51.6 us
  local copies, waits for them, and re-layouts: 20.5 us -> 6.22 us
  other arithmetic: 22.9 us -> 8.94 us
  starting transfers between devices: 23.6 us -> 13.6 us
    ppermute x8 -> x4, waiting for transfers between devices: 2.03 us -> 57.5 us  [passed_along(): return lax.ppermute(block, axis, route)]
    pallas_call x0 -> x3, Pallas kernels: none -> 51.6 us  [the longest x2 26 us: attend_backward(): pl.pallas_call(functools.partial(backward_kernel, c, chunks, ratio), grid...]
    dot_general x7 -> x4, matrix products: 82.2 us -> 42.4 us  [mm(): lax.dot_general(a, b, ((contract[:1], contract[1:]), ((), ())), preferred...]
    sub x1 -> x0, matrix products: 14 us -> none  [attend(): weights = jnp.exp(scores - maximum)]
    convert_element_type x3 -> x2, other arithmetic: 18 us -> 4.29 us  [the longest x1 2.85 us: whole_step(): layer_out = (ours + arrived.astype(jnp.float32)).astype(jnp.bfloat16)]
    ppermute x8 -> x4, starting transfers between devices: 23.4 us -> 10.9 us  [passed_along(): return lax.ppermute(block, axis, route)]
    convert_element_type x5 -> x1, local copies, waits for them, and re-layouts: 6.67 us -> 0.14 us  [whole_step(): theirs.astype(jnp.bfloat16)]
    ppermute x0 -> x2, waiting for transfers between devices: none -> 4.21 us  [swapped(): return lax.ppermute(block, axis, [(0, 1), (1, 0)])]
  transfers between devices with their start and end apart: 11 -> 8, of which waited for: 3 -> 7; matrix products, arithmetic and copies ran while one was open for 33% -> 8% of each run, Pallas kernels for 0% -> 11%
where the time goes in v1:
time: 352 us; the launch traced here: 349 us
  waiting for transfers between devices  212 us (60%)
  Pallas kernels  51.6 us (15%)
  matrix products  42.4 us (12%)
  between operations  14.2 us (4%)
  starting transfers between devices  13.6 us (4%)
  other arithmetic  8.94 us (3%)
  local copies, waits for them, and re-layouts  6.22 us (2%)
    all_gather x2, waiting for transfers between devices, whole_step(): lax.all_gather(out_weight[c * depth:(c + 1) * depth], 'dp', axis=0, tiled...  150 us
    ppermute x4, waiting for transfers between devices, passed_along(): return lax.ppermute(block, axis, route)  57.5 us
    dot_general x4, matrix products, mm(): lax.dot_general(a, b, ((contract[:1], contract[1:]), ((), ())), preferred...  42.4 us
    pallas_call x2, Pallas kernels, attend_backward(): pl.pallas_call(functools.partial(backward_kernel, c, chunks, ratio), grid...  26 us
    pallas_call x1, Pallas kernels, attend_forward(): pl.pallas_call(functools.partial(forward_kernel, chunks, ratio), grid=(gr...  25.6 us
    ppermute x4, starting transfers between devices, passed_along(): return lax.ppermute(block, axis, route)  10.9 us
  transfers between devices with their start and end apart: 8, of which 7 were waited for; matrix products, arithmetic and copies ran while one was open for 8% of the time, Pallas kernels for 11%

profile of v1, /device:TPU:17, one launch (start us, length us, event | category | flops | bytes accessed | tf_op | source)
XLA Modules:
  0.0 349.2 jit_solution(16197690936491585417)
XLA Ops:
  7.3 3.2 fusion
  10.5 0.7 all-gather.5.cloned.1.call-update
  11.3 3.7 %collective-permute-start.1 = (bf16[2,256,512]{2,1,0:T(8,128)(2,1)S(1)}, bf16[2,256,512]{2,1,0:T(8,128)(2,1)S(1)}, u32[]{:S(2)}, u32[]{:S(2)}) collective-permute-start(bf16[2,256,512]{2,1,0:T(8,128)(2,1)S(1)} %pad_maximum_fusion), channel_id=1, source_target_pairs={{0,2},{2,4},{4,6},{6,8},{8,10},{10,12},{12,14},{14,16},{16,18},{18... | collective-permute-start | bytes 1572872 | tf_op jit(solution)/shard_map/ppermute | solution.py:19
  15.0 3.2 collective-permute-start
  18.2 1.3 collective-permute-start.2
  19.6 0.1 reduce
  19.8 0.1 select_reduce_fusion
  19.9 0.6 broadcast_subtract_fusion
  20.4 6.9 %collective-permute-done.1 = bf16[2,256,512]{2,1,0:T(8,128)(2,1)S(1)} collective-permute-done((bf16[2,256,512]{2,1,0:T(8,128)(2,1)S(1)}, bf16[2,256,512]{2,1,0:T(8,128)(2,1)S(1)}, u32[]{:S(2)}, u32[]{:S(2)}) %collective-permute-start.1) | collective-permute-done | bytes 524320 | tf_op jit(solution)/shard_map/ppermute | solution.py:19
  27.3 34.3 %collective-permute-done = bf16[2,256,512]{2,1,0:T(8,128)(2,1)S(1)} collective-permute-done((bf16[2,256,512]{2,1,0:T(8,128)(2,1)S(1)}, bf16[2,256,512]{2,1,0:T(8,128)(2,1)S(1)}, u32[]{:S(2)}, u32[]{:S(2)}) %collective-permute-start) | collective-permute-done | bytes 524320 | tf_op jit(solution)/shard_map/ppermute | solution.py:19
  61.6 1.3 maximum_maximum_fusion.kv_ref.refs_1_
  62.9 25.6 %attend_forward.1 = (bf16[256,2048]{1,0:T(8,128)(2,1)}, bf16[256,2048]{1,0:T(8,128)(2,1)}, bf16[2,4,4,768,256]{4,3,2,1,0:T(8,128)(2,1)}) custom-call(s32[1,256]{1,0:T(1,128)} %bitcast.21, bf16[256,4096]{1,0:T(8,128)(2,1)} %refs_0_.3, bf16[2,768,512]{2,1,0:T(8,128)(2,1)} %maximum_maximum_fusion.kv_ref.refs_1_), custom_call_target="tpu_custom_call" | custom-call | flops 6442450944 | bytes 12582912 | tf_op jit(solution)/shard_map/attend_forward/pallas_call | solution.py:62
  88.5 2.5 maximum_select_fusion
  91.0 57.4 %all-gather.3.cloned.1.call-done = bf16[2048,4096]{1,0:T(8,128)(2,1)} async-done(((bf16[128,4096]{1,0:T(8,128)(2,1)}), bf16[2048,4096]{1,0:T(8,128)(2,1)}) %all-gather.3.cloned.1.call-update) | async-done | bytes 16777232 | tf_op jit(solution)/shard_map/all_gather | solution.py:178
  148.4 9.3 %convolution_convert_fusion.1.refs_3_ = bf16[256,2048]{1,0:T(8,128)(2,1)} fusion(bf16[256,4096]{1,0:T(8,128)(2,1)S(1)} %maximum_select_fusion, bf16[2048,4096]{1,0:T(8,128)(2,1)} %all-gather.3.cloned.1.call-done), kind=kOutput, calls=%fused_computation.2 | convolution fusion | flops 4295491584 | bytes 19922944 | tf_op jit(solution)/shard_map/dot_general | solution.py:33
  157.7 12.9 %shard_map.93 = (bf16[256,2048]{1,0:T(8,128)(2,1)}, f32[2,768,512]{2,1,0:T(8,128)}) custom-call(bf16[256,4096]{1,0:T(8,128)(2,1)} %refs_0_.3, bf16[2,768,512]{2,1,0:T(8,128)(2,1)} %maximum_maximum_fusion.kv_ref.refs_1_, bf16[2,4,4,768,256]{4,3,2,1,0:T(8,128)(2,1)} %get-tuple-element.19.refs_2_, bf16[256,2048]{1,0:T(8,128)(2,1)} %convolution_convert_fusion.1.refs_3_, ...), custom_call_target="tpu_custom_call" | custom-call | flops 6442450944 | bytes 6291456 | tf_op jit(solution)/shard_map/pallas_call | solution.py:144
  170.6 12.7 %fusion.1 = f32[256,4096]{1,0:T(8,128)} fusion(bf16[256,2048]{1,0:T(8,128)(2,1)} %get-tuple-element.20.refs_4_, bf16[2048,4096]{1,0:T(8,128)(2,1)} %all-gather.3.cloned.1.call-done), kind=kOutput, calls=%fused_computation.15 | convolution fusion | flops 4294967296 | bytes 22020096 | tf_op jit(solution)/shard_map/dot_general | solution.py:33
  183.3 92.5 %all-gather.5.cloned.1.call-done = bf16[2048,4096]{1,0:T(8,128)(2,1)} async-done(((bf16[128,4096]{1,0:T(8,128)(2,1)}), bf16[2048,4096]{1,0:T(8,128)(2,1)}) %all-gather.5.cloned.1.call-update) | async-done | bytes 16777232 | tf_op jit(solution)/shard_map/all_gather | solution.py:178
  275.8 11.2 %convolution_add_fusion = f32[256,4096]{1,0:T(8,128)S(1)} fusion(f32[256,4096]{1,0:T(8,128)} %fusion.1, bf16[256,2048]{1,0:T(8,128)(2,1)S(1)} %copy-done.5, bf16[2048,4096]{1,0:T(8,128)(2,1)} %all-gather.5.cloned.1.call-done), kind=kOutput, calls=%fused_computation | convolution fusion | flops 4296015872 | bytes 26214400 | tf_op jit(solution)/shard_map/dot_general | solution.py:33
  287.0 1.9 copy-done
  288.9 0.1 dynamic-slice_convert_fusion
  289.1 9.2 %convolution_convert_fusion.refs_3_ = bf16[256,2048]{1,0:T(8,128)(2,1)} fusion(bf16[256,4096]{1,0:T(8,128)(2,1)S(1)} %maximum_select_fusion, bf16[2048,4096]{1,0:T(8,128)(2,1)} %all-gather.5.cloned.1.call-done), kind=kOutput, calls=%fused_computation.1 | convolution fusion | flops 4295491584 | bytes 19922944 | tf_op jit(solution)/shard_map/dot_general | solution.py:33
  298.3 13.0 %shard_map.94 = (bf16[256,4096]{1,0:T(8,128)(2,1)}, f32[2,256,512]{2,1,0:T(8,128)}, bf16[2,256,512]{2,1,0:T(8,128)(2,1)}, bf16[2,256,512]{2,1,0:T(8,128)(2,1)}) custom-call(bf16[256,4096]{1,0:T(8,128)(2,1)} %refs_0_.3, bf16[2,768,512]{2,1,0:T(8,128)(2,1)} %maximum_maximum_fusion.kv_ref.refs_1_, bf16[2,4,4,768,256]{4,3,2,1,0:T(8,128)(2,1)} %get-tuple-element.19.refs_2_, ...), custom_call_target="tpu_custom_call" | custom-call | flops 6442450944 | bytes 6291456 | tf_op jit(solution)/shard_map/pallas_call | solution.py:144
  311.4 1.9 collective-permute-start.5
  313.3 2.2 collective-permute-start.4
  315.5 1.3 collective-permute-start.3
  316.7 10.0 %collective-permute-done.5 = bf16[2,256,512]{2,1,0:T(8,128)(2,1)S(1)} collective-permute-done((bf16[2,256,512]{2,1,0:T(8,128)(2,1)}, bf16[2,256,512]{2,1,0:T(8,128)(2,1)S(1)}, u32[]{:S(2)}, u32[]{:S(2)}) %collective-permute-start.5) | collective-permute-done | bytes 524320 | tf_op jit(solution)/shard_map/ppermute | solution.py:19
  326.7 6.3 %collective-permute-done.4 = bf16[2,256,512]{2,1,0:T(8,128)(2,1)S(1)} collective-permute-done((bf16[2,256,512]{2,1,0:T(8,128)(2,1)}, bf16[2,256,512]{2,1,0:T(8,128)(2,1)S(1)}, u32[]{:S(2)}, u32[]{:S(2)}) %collective-permute-start.4) | collective-permute-done | bytes 524320 | tf_op jit(solution)/shard_map/ppermute | solution.py:19
  333.0 1.4 add_convert_fusion.1
  334.5 0.8 slice_bitcast_fusion
  335.3 4.2 %collective-permute-done.3 = bf16[256,2048]{1,0:T(8,128)(2,1)S(1)} collective-permute-done((bf16[256,2048]{1,0:T(8,128)(2,1)S(1)}, bf16[256,2048]{1,0:T(8,128)(2,1)S(1)}, u32[]{:S(2)}, u32[]{:S(2)}) %collective-permute-start.3) | collective-permute-done | bytes 1048608 | tf_op jit(solution)/shard_map/ppermute | solution.py:23
  339.5 2.9 add_convert_fusion
  (19 shorter events, 0.3 us)
Async XLA Ops:
  7.2 4.1 %copy-start.2 = (bf16[256,512]{1,0:T(8,128)(2,1)S(1)}, bf16[256,512]{1,0:T(8,128)(2,1)}, u32[]{:S(2)}) copy-start(bf16[256,512]{1,0:T(8,128)(2,1)} %param.8) | copy-start | bytes 786436
  7.2 4.1 %copy-start.3 = (bf16[256,512]{1,0:T(8,128)(2,1)S(1)}, bf16[256,512]{1,0:T(8,128)(2,1)}, u32[]{:S(2)}) copy-start(bf16[256,512]{1,0:T(8,128)(2,1)} %param.7) | copy-start | bytes 786436
  7.2 11.0 %copy-start.1 = (bf16[256,2048]{1,0:T(8,128)(2,1)S(1)}, bf16[256,2048]{1,0:T(8,128)(2,1)}, u32[]{:S(2)}) copy-start(bf16[256,2048]{1,0:T(8,128)(2,1)} %param.9) | copy-start | bytes 3145732
  7.2 12.3 %copy-start.4 = (s32[16]{0:T(128)S(1)}, s32[16]{0:T(128)}, u32[]{:S(2)}) copy-start(s32[16]{0:T(128)} %param.11) | copy-start | bytes 196
  7.2 141.2 %all-gather.3.cloned.1.call-start = ((), (), s32[]{:S(2)}) async-start(), calls=%async_computation | async-start | bytes 17825792 | tf_op jit(solution)/shard_map/all_gather | solution.py:178
  10.5 265.3 %all-gather.5.cloned.1.call-start = ((), (), s32[]{:S(2)}) async-start(), calls=%async_computation.1 | async-start | bytes 17825792 | tf_op jit(solution)/shard_map/all_gather | solution.py:178
  11.3 16.0 %collective-permute-start.1 = (bf16[2,256,512]{2,1,0:T(8,128)(2,1)S(1)}, bf16[2,256,512]{2,1,0:T(8,128)(2,1)S(1)}, u32[]{:S(2)}, u32[]{:S(2)}) collective-permute-start(bf16[2,256,512]{2,1,0:T(8,128)(2,1)S(1)} %pad_maximum_fusion), channel_id=1, source_target_pairs={{0,2},{2,4},{4,6},{6,8},{8,10},{10,12},{12,14},{14,16},{16,18},{18... | collective-permute-start | bytes 1572872 | tf_op jit(solution)/shard_map/ppermute | solution.py:19
  15.0 46.6 %collective-permute-start = (bf16[2,256,512]{2,1,0:T(8,128)(2,1)S(1)}, bf16[2,256,512]{2,1,0:T(8,128)(2,1)S(1)}, u32[]{:S(2)}, u32[]{:S(2)}) collective-permute-start(bf16[2,256,512]{2,1,0:T(8,128)(2,1)S(1)} %pad_maximum_fusion), channel_id=1, source_target_pairs={{0,4},{2,6},{4,8},{6,10},{8,12},{10,14},{12,16},{14,18},{16,20},{1... | collective-permute-start | bytes 1572872 | tf_op jit(solution)/shard_map/ppermute | solution.py:19
  18.2 70.2 %collective-permute-start.2 = (bf16[256,2048]{1,0:T(8,128)(2,1)S(1)}, bf16[256,2048]{1,0:T(8,128)(2,1)}, u32[]{:S(2)}, u32[]{:S(2)}) collective-permute-start(bf16[256,2048]{1,0:T(8,128)(2,1)S(1)} %copy-done.1), channel_id=1, source_target_pairs={{0,1},{1,0},{2,3},{3,2},{4,5},{5,4},{6,7},{7,6},{8,9},{9,8},{10,11... | collective-permute-start | bytes 3145736 | tf_op jit(solution)/shard_map/ppermute | solution.py:23
  170.6 105.2 %copy-start.5 = (bf16[256,2048]{1,0:T(8,128)(2,1)S(1)}, bf16[256,2048]{1,0:T(8,128)(2,1)}, u32[]{:S(2)}) copy-start(bf16[256,2048]{1,0:T(8,128)(2,1)} %get-tuple-element.24.refs_4_) | copy-start | bytes 3145732
  287.0 1.9 copy-start
  311.4 15.3 %collective-permute-start.5 = (bf16[2,256,512]{2,1,0:T(8,128)(2,1)}, bf16[2,256,512]{2,1,0:T(8,128)(2,1)S(1)}, u32[]{:S(2)}, u32[]{:S(2)}) collective-permute-start(bf16[2,256,512]{2,1,0:T(8,128)(2,1)} %get-tuple-element.33), channel_id=1, source_target_pairs={{4,0},{6,2},{8,4},{10,6},{12,8},{14,10},{16,12},{18,14},{20,16},{2... | collective-permute-start | bytes 1572872 | tf_op jit(solution)/shard_map/ppermute | solution.py:19
  313.3 19.7 %collective-permute-start.4 = (bf16[2,256,512]{2,1,0:T(8,128)(2,1)}, bf16[2,256,512]{2,1,0:T(8,128)(2,1)S(1)}, u32[]{:S(2)}, u32[]{:S(2)}) collective-permute-start(bf16[2,256,512]{2,1,0:T(8,128)(2,1)} %get-tuple-element.32), channel_id=1, source_target_pairs={{2,0},{4,2},{6,4},{8,6},{10,8},{12,10},{14,12},{16,14},{18,16},{20... | collective-permute-start | bytes 1572872 | tf_op jit(solution)/shard_map/ppermute | solution.py:19
  315.5 24.0 %collective-permute-start.3 = (bf16[256,2048]{1,0:T(8,128)(2,1)S(1)}, bf16[256,2048]{1,0:T(8,128)(2,1)S(1)}, u32[]{:S(2)}, u32[]{:S(2)}) collective-permute-start(bf16[256,2048]{1,0:T(8,128)(2,1)S(1)} %dynamic-slice_convert_fusion), channel_id=1, source_target_pairs={{0,1},{1,0},{2,3},{3,2},{4,5},{5,4},{6,7},{7,6},{8,9},{9,8},{10,11... | collective-permute-start | bytes 3145736 | tf_op jit(solution)/shard_map/ppermute | solution.py:23
Sparse Core Ops, SparseCore 0:
  10.6 137.7 all-gather.2
  151.1 124.5 all-gather.4

commit v2 on v1

--- a/solution.py
+++ b/solution.py
@@ -168,16 +168,8 @@
     side = lax.axis_index("head")
     two_sided = lax.axis_size("head") == 2
     own_width = output_grad.shape[1]
-    ratio = queries.shape[1] // keys.shape[1]
-    chunks = out_weight.shape[0] // HD if out_weight.shape[0] % HD == 0 else 1
-    if chunks == 0 or ratio % chunks:
-        chunks = 1
-    depth = out_weight.shape[0] // chunks
-
-    weights = [
-        lax.all_gather(out_weight[c * depth : (c + 1) * depth], "dp", axis=0, tiled=True)
-        for c in range(chunks)
-    ]
+    depth = out_weight.shape[0]
+    held = out_weight
     couple = jnp.stack([keys, values])
     earlier = [passed_along(couple, "dp", offset) for offset in range(1, SPAN + 1)]
     kv = jnp.concatenate(earlier[::-1] + [couple], axis=1)
@@ -193,30 +185,47 @@
 
     positions = device * block_rows + jnp.arange(block_rows, dtype=jnp.int32)
     starts = doc_start(lengths, positions) - (device - SPAN) * block_rows
-    *attended, shares = attend_forward(starts[None, :], queries, kv, chunks)
-
-    projected = None
-    query_parts, total = [], None
-    for c in range(chunks):
-        d_attended = mm(upstream_all, weights[c], (1, 1)).astype(jnp.bfloat16)
-        part = mm(attended[c], weights[c], (1, 0))
-        projected = part if projected is None else projected + part
-        if c == chunks - 1:
-            if two_sided:
-                theirs = lax.dynamic_slice_in_dim(projected, (1 - side) * own_width, own_width, 1)
-                ours = lax.dynamic_slice_in_dim(projected, side * own_width, own_width, 1)
-            else:
-                theirs, ours = projected, projected
-            d_attended, theirs = lax.optimization_barrier((d_attended, theirs.astype(jnp.bfloat16)))
-        passed = query_parts + [total] if c > 0 else []
-        query_grad, *sums = attend_backward(
-            c, chunks, queries, kv, shares, d_attended, attended[c], passed
-        )
-        if c < chunks - 1:
-            query_parts.append(query_grad)
-            total, projected, upstream_all, attended[c + 1] = lax.optimization_barrier(
-                (sums[0], projected, upstream_all, attended[c + 1])
-            )
+    attended, shares = attend_forward(starts[None, :], queries, kv, 1)
+
+    if two_sided:
+        chips = lax.axis_size("dp") // 2
+        cycle = list(range(0, chips, 2)) + list(range(chips - 1, 0, -2))
+        place_of = jnp.array([cycle.index(chip) for chip in range(chips)], jnp.int32)
+        chip_at = jnp.array(cycle, jnp.int32)
+        onward = []
+        for r, chip in enumerate(cycle):
+            onward.append((2 * chip, 2 * cycle[(r + 1) % chips]))
+            onward.append((2 * chip + 1, 2 * cycle[(r - 1) % chips] + 1))
+        partner = [(i, i ^ 1) for i in range(2 * chips)]
+        place, core = place_of[device // 2], device % 2
+        d_attended = jnp.zeros((block_rows, queries.shape[1]), jnp.bfloat16)
+        projected = jnp.zeros((block_rows, upstream_all.shape[1]), jnp.float32)
+        for step in range(chips):
+            paired = lax.ppermute(held, "dp", partner)
+            following = held
+            if step < chips - 1:
+                following = lax.ppermute(held, "dp", onward)
+            up = 2 * chip_at[(place - step) % chips]
+            down = 2 * chip_at[(place + step) % chips] + 1
+            for block, owner in (
+                (held, jnp.where(core == 0, up, down)),
+                (paired, jnp.where(core == 0, down, up)),
+            ):
+                part = mm(upstream_all, block, (1, 1)).astype(jnp.bfloat16)
+                d_attended = lax.dynamic_update_slice_in_dim(d_attended, part, owner * depth, 1)
+                columns = lax.dynamic_slice_in_dim(attended, owner * depth, depth, 1)
+                projected = projected + mm(columns, block, (1, 0))
+            held = following
+        theirs = lax.dynamic_slice_in_dim(projected, (1 - side) * own_width, own_width, 1)
+        ours = lax.dynamic_slice_in_dim(projected, side * own_width, own_width, 1)
+    else:
+        weights = lax.all_gather(out_weight, "dp", axis=0, tiled=True)
+        d_attended = mm(upstream_all, weights, (1, 1)).astype(jnp.bfloat16)
+        ours = theirs = mm(attended, weights, (1, 0))
+    d_attended, theirs = lax.optimization_barrier((d_attended, theirs.astype(jnp.bfloat16)))
+    query_grad, *sums = attend_backward(
+        0, 1, queries, kv, shares, d_attended, attended, []
+    )
 
     if two_sided:
         arrived = swapped(theirs, "head")

time: 352 us -> 295 us (0.84)
  waiting for transfers between devices: 212 us -> 92.9 us
  starting transfers between devices: 13.6 us -> 66.6 us
  between operations: 14.2 us -> 21.9 us
  Pallas kernels: 51.6 us -> 47.8 us
    all_gather x2 -> x0, waiting for transfers between devices: 150 us -> none  [whole_step(): lax.all_gather(out_weight[c * depth:(c + 1) * depth], 'dp', axis=0, tiled...]
    ppermute x0 -> x15, waiting for transfers between devices: none -> 72.5 us  [the longest x7 72.4 us: whole_step(): following = lax.ppermute(held, 'dp', onward)]
    ppermute x0 -> x15, starting transfers between devices: none -> 49.6 us  [the longest x8 46.7 us: whole_step(): paired = lax.ppermute(held, 'dp', partner)]
    ppermute x4, waiting for transfers between devices: 57.5 us -> 11.9 us  [passed_along(): return lax.ppermute(block, axis, route)]
    ppermute x2, waiting for transfers between devices: 4.21 us -> 8.55 us  [swapped(): return lax.ppermute(block, axis, [(0, 1), (1, 0)])]
    pallas_call x2 -> x1, Pallas kernels: 26 us -> 22.3 us  [attend_backward(): pl.pallas_call(functools.partial(backward_kernel, c, chunks, ratio), grid...]
    dot_general x4 -> x32, matrix products: 42.4 us -> 45.5 us  [mm(): lax.dot_general(a, b, ((contract[:1], contract[1:]), ((), ())), preferred...]
  transfers between devices with their start and end apart: 8 -> 21, of which waited for: 7 -> 9; matrix products, arithmetic and copies ran while one was open for 8% -> 19% of each run, Pallas kernels for 11% -> 9%
where the time goes in v2:
time: 295 us; the launch traced here: 292 us
  waiting for transfers between devices  92.9 us (31%)
  starting transfers between devices  66.6 us (23%)
  Pallas kernels  47.8 us (16%)
  matrix products  45.5 us (15%)
  between operations  21.9 us (7%)
  other arithmetic  9.12 us (3%)
  local copies, waits for them, and re-layouts  8.43 us (3%)
    ppermute x7, waiting for transfers between devices, whole_step(): following = lax.ppermute(held, 'dp', onward)  72.4 us
    ppermute x8, starting transfers between devices, whole_step(): paired = lax.ppermute(held, 'dp', partner)  46.7 us
    dot_general x32, matrix products, mm(): lax.dot_general(a, b, ((contract[:1], contract[1:]), ((), ())), preferred...  45.5 us
    pallas_call x1, Pallas kernels, attend_forward(): pl.pallas_call(functools.partial(forward_kernel, chunks, ratio), grid=(gr...  25.5 us
    pallas_call x1, Pallas kernels, attend_backward(): pl.pallas_call(functools.partial(backward_kernel, c, chunks, ratio), grid...  22.3 us
    ppermute x4, starting transfers between devices, passed_along(): return lax.ppermute(block, axis, route)  14.4 us
    ppermute x4, waiting for transfers between devices, passed_along(): return lax.ppermute(block, axis, route)  11.9 us
    ppermute x2, waiting for transfers between devices, swapped(): return lax.ppermute(block, axis, [(0, 1), (1, 0)])  8.55 us
  transfers between devices with their start and end apart: 21, of which 9 were waited for; matrix products, arithmetic and copies ran while one was open for 19% of the time, Pallas kernels for 9%

profile of v2, /device:TPU:17, one launch (start us, length us, event | category | flops | bytes accessed | tf_op | source)
XLA Modules:
  0.0 292.3 jit_solution(15136875408707338453)
XLA Ops:
  0.9 25.3 %collective-permute-done.3 = bf16[256,4096]{1,0:T(8,128)(2,1)} collective-permute-done((bf16[256,4096]{1,0:T(8,128)(2,1)}, bf16[256,4096]{1,0:T(8,128)(2,1)}, u32[]{:S(2)}, u32[]{:S(2)}) %collective-permute-start.3) | collective-permute-done | bytes 2097184 | tf_op jit(solution)/shard_map/ppermute | solution.py:207
  27.4 4.2 %collective-permute-start = (bf16[2,256,512]{2,1,0:T(8,128)(2,1)S(1)}, bf16[2,256,512]{2,1,0:T(8,128)(2,1)S(1)}, u32[]{:S(2)}, u32[]{:S(2)}) collective-permute-start(bf16[2,256,512]{2,1,0:T(8,128)(2,1)S(1)} %pad_maximum_fusion), channel_id=1, source_target_pairs={{0,4},{2,6},{4,8},{6,10},{8,12},{10,14},{12,16},{14,18},{16,20},{1... | collective-permute-start | bytes 1572872 | tf_op jit(solution)/shard_map/ppermute | solution.py:19
  31.7 5.1 %collective-permute-start.1 = (bf16[2,256,512]{2,1,0:T(8,128)(2,1)S(1)}, bf16[2,256,512]{2,1,0:T(8,128)(2,1)S(1)}, u32[]{:S(2)}, u32[]{:S(2)}) collective-permute-start(bf16[2,256,512]{2,1,0:T(8,128)(2,1)S(1)} %pad_maximum_fusion), channel_id=1, source_target_pairs={{0,2},{2,4},{4,6},{6,8},{8,10},{10,12},{12,14},{14,16},{16,18},{18... | collective-permute-start | bytes 1572872 | tf_op jit(solution)/shard_map/ppermute | solution.py:19
  50.7 2.0 fusion.61
  64.6 2.3 maximum_maximum_fusion.kv_ref.refs_1_
  66.9 25.5 %attend_forward.1 = (bf16[256,4096]{1,0:T(8,128)(2,1)}, bf16[1,4,8,768,256]{4,3,2,1,0:T(8,128)(2,1)}) custom-call(s32[1,256]{1,0:T(1,128)} %bitcast.61, bf16[256,4096]{1,0:T(8,128)(2,1)} %refs_0_.1, bf16[2,768,512]{2,1,0:T(8,128)(2,1)} %maximum_maximum_fusion.kv_ref.refs_1_), custom_call_target="tpu_custom_call" | custom-call | flops 6442450944 | bytes 12582912 | tf_op jit(solution)/shard_map/attend_forward/pallas_call | solution.py:62
  92.7 1.6 fusion.43
  97.4 6.6 %collective-permute-start.4 = (bf16[256,4096]{1,0:T(8,128)(2,1)}, bf16[256,4096]{1,0:T(8,128)(2,1)S(1)}, u32[]{:S(2)}, u32[]{:S(2)}) collective-permute-start(bf16[256,4096]{1,0:T(8,128)(2,1)} %collective-permute-done.3), channel_id=1, source_target_pairs={{0,2},{2,0},{4,6},{6,4},{8,10},{10,8},{12,14},{14,12},{16,18},{18,... | collective-permute-start | bytes 6291464 | tf_op jit(solution)/shard_map/ppermute | solution.py:204
  104.0 3.1 %fusion.20 = bf16[256,4096]{1,0:T(8,128)(2,1)} fusion(bf16[256,4096]{1,0:T(8,128)(2,1)} %fusion.21, s32[]{:T(128)S(6)} %select_n.261, bf16[256,4096]{1,0:T(8,128)(2,1)} %collective-permute-done.2, bf16[256,2048]{1,0:T(8,128)(2,1)S(1)} %collective-permute-done.17, bf16[256,2048]{1,0:T(8,128)(2,1)S(1)} %copy-done.3, pred[]{:T(512)S(6)} %eq.40), kind=kOutput, calls=%fused_computation.48 | convolution fusion | flops 546373632 | bytes 4325381 | tf_op jit(solution)/shard_map/dot_general | solution.py:33
  107.1 2.4 convolution_add_fusion.8
  109.5 2.4 convolution_add_fusion.7
  111.9 6.0 %collective-permute-done.7 = bf16[256,4096]{1,0:T(8,128)(2,1)S(1)} collective-permute-done((bf16[256,4096]{1,0:T(8,128)(2,1)}, bf16[256,4096]{1,0:T(8,128)(2,1)S(1)}, u32[]{:S(2)}, u32[]{:S(2)}) %collective-permute-start.7) | collective-permute-done | bytes 2097184 | tf_op jit(solution)/shard_map/ppermute | solution.py:207
  118.9 3.1 %fusion.19 = bf16[256,4096]{1,0:T(8,128)(2,1)} fusion(bf16[256,4096]{1,0:T(8,128)(2,1)} %fusion.20, s32[]{:T(128)S(6)} %select_n.267, bf16[256,4096]{1,0:T(8,128)(2,1)} %collective-permute-done.3, bf16[256,2048]{1,0:T(8,128)(2,1)S(1)} %collective-permute-done.17, bf16[256,2048]{1,0:T(8,128)(2,1)S(1)} %copy-done.3, pred[]{:T(512)S(6)} %eq.40), kind=kOutput, calls=%fused_computation.46 | convolution fusion | flops 546373632 | bytes 4325381 | tf_op jit(solution)/shard_map/dot_general | solution.py:33
  122.0 6.7 %collective-permute-start.6 = (bf16[256,4096]{1,0:T(8,128)(2,1)}, bf16[256,4096]{1,0:T(8,128)(2,1)S(1)}, u32[]{:S(2)}, u32[]{:S(2)}) collective-permute-start(bf16[256,4096]{1,0:T(8,128)(2,1)} %collective-permute-done.5), channel_id=1, source_target_pairs={{0,2},{2,0},{4,6},{6,4},{8,10},{10,8},{12,14},{14,12},{16,18},{18,... | collective-permute-start | bytes 6291464 | tf_op jit(solution)/shard_map/ppermute | solution.py:204
  128.7 2.3 fusion.38
  133.3 3.1 %fusion.17 = bf16[256,4096]{1,0:T(8,128)(2,1)} fusion(bf16[256,4096]{1,0:T(8,128)(2,1)} %fusion.18, s32[]{:T(128)S(6)} %select_n.275, bf16[256,4096]{1,0:T(8,128)(2,1)} %collective-permute-done.5, bf16[256,2048]{1,0:T(8,128)(2,1)S(1)} %collective-permute-done.17, bf16[256,2048]{1,0:T(8,128)(2,1)S(1)} %copy-done.3, pred[]{:T(512)S(6)} %eq.40), kind=kOutput, calls=%fused_computation.42 | convolution fusion | flops 546373632 | bytes 4325381 | tf_op jit(solution)/shard_map/dot_general | solution.py:33
  136.4 6.6 %collective-permute-done.9 = bf16[256,4096]{1,0:T(8,128)(2,1)S(1)} collective-permute-done((bf16[256,4096]{1,0:T(8,128)(2,1)S(1)}, bf16[256,4096]{1,0:T(8,128)(2,1)S(1)}, u32[]{:S(2)}, u32[]{:S(2)}) %collective-permute-start.9) | collective-permute-done | bytes 2097184 | tf_op jit(solution)/shard_map/ppermute | solution.py:207
  147.0 7.6 %collective-permute-start.10 = (bf16[256,4096]{1,0:T(8,128)(2,1)S(1)}, bf16[256,4096]{1,0:T(8,128)(2,1)S(1)}, u32[]{:S(2)}, u32[]{:S(2)}) collective-permute-start(bf16[256,4096]{1,0:T(8,128)(2,1)S(1)} %collective-permute-done.9), channel_id=1, source_target_pairs={{0,2},{2,0},{4,6},{6,4},{8,10},{10,8},{12,14},{14,12},{16,18},{18,... | collective-permute-start | bytes 6291464 | tf_op jit(solution)/shard_map/ppermute | solution.py:204
  157.5 11.9 %collective-permute-done.11 = bf16[256,4096]{1,0:T(8,128)(2,1)S(1)} collective-permute-done((bf16[256,4096]{1,0:T(8,128)(2,1)S(1)}, bf16[256,4096]{1,0:T(8,128)(2,1)S(1)}, u32[]{:S(2)}, u32[]{:S(2)}) %collective-permute-start.11) | collective-permute-done | bytes 2097184 | tf_op jit(solution)/shard_map/ppermute | solution.py:207
  172.3 8.3 %collective-permute-start.12 = (bf16[256,4096]{1,0:T(8,128)(2,1)S(1)}, bf16[256,4096]{1,0:T(8,128)(2,1)S(1)}, u32[]{:S(2)}, u32[]{:S(2)}) collective-permute-start(bf16[256,4096]{1,0:T(8,128)(2,1)S(1)} %collective-permute-done.11), channel_id=1, source_target_pairs={{0,2},{2,0},{4,6},{6,4},{8,10},{10,8},{12,14},{14,12},{16,18},{18,... | collective-permute-start | bytes 6291464 | tf_op jit(solution)/shard_map/ppermute | solution.py:204
  183.5 11.1 %collective-permute-done.13 = bf16[256,4096]{1,0:T(8,128)(2,1)S(1)} collective-permute-done((bf16[256,4096]{1,0:T(8,128)(2,1)S(1)}, bf16[256,4096]{1,0:T(8,128)(2,1)S(1)}, u32[]{:S(2)}, u32[]{:S(2)}) %collective-permute-start.13) | collective-permute-done | bytes 2097184 | tf_op jit(solution)/shard_map/ppermute | solution.py:207
  196.1 9.2 %collective-permute-start.14 = (bf16[256,4096]{1,0:T(8,128)(2,1)S(1)}, bf16[256,4096]{1,0:T(8,128)(2,1)S(1)}, u32[]{:S(2)}, u32[]{:S(2)}) collective-permute-start(bf16[256,4096]{1,0:T(8,128)(2,1)S(1)} %collective-permute-done.13), channel_id=1, source_target_pairs={{0,2},{2,0},{4,6},{6,4},{8,10},{10,8},{12,14},{14,12},{16,18},{18,... | collective-permute-start | bytes 6291464 | tf_op jit(solution)/shard_map/ppermute | solution.py:204
  208.2 11.6 %collective-permute-done.15 = bf16[256,4096]{1,0:T(8,128)(2,1)S(1)} collective-permute-done((bf16[256,4096]{1,0:T(8,128)(2,1)S(1)}, bf16[256,4096]{1,0:T(8,128)(2,1)S(1)}, u32[]{:S(2)}, u32[]{:S(2)}) %collective-permute-start.15) | collective-permute-done | bytes 2097184 | tf_op jit(solution)/shard_map/ppermute | solution.py:207
  219.8 8.2 %collective-permute-start.16 = (bf16[256,4096]{1,0:T(8,128)(2,1)S(1)}, bf16[256,4096]{1,0:T(8,128)(2,1)S(1)}, u32[]{:S(2)}, u32[]{:S(2)}) collective-permute-start(bf16[256,4096]{1,0:T(8,128)(2,1)S(1)} %collective-permute-done.15), channel_id=1, source_target_pairs={{0,2},{2,0},{4,6},{6,4},{8,10},{10,8},{12,14},{14,12},{16,18},{18,... | collective-permute-start | bytes 6291464 | tf_op jit(solution)/shard_map/ppermute | solution.py:204
  234.5 1.9 copy-done
  238.0 22.3 %shard_map.111 = (bf16[256,4096]{1,0:T(8,128)(2,1)}, f32[2,256,512]{2,1,0:T(8,128)}, bf16[2,256,512]{2,1,0:T(8,128)(2,1)}, bf16[2,256,512]{2,1,0:T(8,128)(2,1)}) custom-call(bf16[256,4096]{1,0:T(8,128)(2,1)} %refs_0_.1, bf16[2,768,512]{2,1,0:T(8,128)(2,1)} %maximum_maximum_fusion.kv_ref.refs_1_, bf16[1,4,8,768,256]{4,3,2,1,0:T(8,128)(2,1)} %get-tuple-element.14.refs_2_, ...), custom_call_target="tpu_custom_call" | custom-call | flops 12884901888 | bytes 12582912 | tf_op jit(solution)/shard_map/pallas_call | solution.py:144
  260.3 1.9 collective-permute-start.19
  262.3 3.2 %collective-permute-start.20 = (bf16[2,256,512]{2,1,0:T(8,128)(2,1)}, bf16[2,256,512]{2,1,0:T(8,128)(2,1)S(1)}, u32[]{:S(2)}, u32[]{:S(2)}) collective-permute-start(bf16[2,256,512]{2,1,0:T(8,128)(2,1)} %get-tuple-element.19), channel_id=1, source_target_pairs={{4,0},{6,2},{8,4},{10,6},{12,8},{14,10},{16,12},{18,14},{20,16},{2... | collective-permute-start | bytes 1572872 | tf_op jit(solution)/shard_map/ppermute | solution.py:19
  266.7 8.5 %collective-permute-done.19 = bf16[2,256,512]{2,1,0:T(8,128)(2,1)S(1)} collective-permute-done((bf16[2,256,512]{2,1,0:T(8,128)(2,1)}, bf16[2,256,512]{2,1,0:T(8,128)(2,1)S(1)}, u32[]{:S(2)}, u32[]{:S(2)}) %collective-permute-start.19) | collective-permute-done | bytes 524320 | tf_op jit(solution)/shard_map/ppermute | solution.py:19
  275.2 3.5 %collective-permute-done.20 = bf16[2,256,512]{2,1,0:T(8,128)(2,1)S(1)} collective-permute-done((bf16[2,256,512]{2,1,0:T(8,128)(2,1)}, bf16[2,256,512]{2,1,0:T(8,128)(2,1)S(1)}, u32[]{:S(2)}, u32[]{:S(2)}) %collective-permute-start.20) | collective-permute-done | bytes 524320 | tf_op jit(solution)/shard_map/ppermute | solution.py:19
  280.9 8.5 %collective-permute-done.18 = bf16[256,2048]{1,0:T(8,128)(2,1)S(1)} collective-permute-done((bf16[256,2048]{1,0:T(8,128)(2,1)S(1)}, bf16[256,2048]{1,0:T(8,128)(2,1)S(1)}, u32[]{:S(2)}, u32[]{:S(2)}) %collective-permute-start.18) | collective-permute-done | bytes 1048608 | tf_op jit(solution)/shard_map/ppermute | solution.py:23
  289.5 2.9 add_convert_fusion
  (67 shorter events, 41.7 us)
Async XLA Ops:
  0.6 25.5 %collective-permute-start.3 = (bf16[256,4096]{1,0:T(8,128)(2,1)}, bf16[256,4096]{1,0:T(8,128)(2,1)}, u32[]{:S(2)}, u32[]{:S(2)}) collective-permute-start(bf16[256,4096]{1,0:T(8,128)(2,1)} %param.12), channel_id=1, source_target_pairs={{0,8},{2,6},{8,16},{10,2},{16,24},{18,10},{24,28},{26,18},{28,20},... | collective-permute-start | bytes 6291464 | tf_op jit(solution)/shard_map/ppermute | solution.py:207
  26.2 66.2 %collective-permute-start.5 = (bf16[256,4096]{1,0:T(8,128)(2,1)}, bf16[256,4096]{1,0:T(8,128)(2,1)}, u32[]{:S(2)}, u32[]{:S(2)}) collective-permute-start(bf16[256,4096]{1,0:T(8,128)(2,1)} %collective-permute-done.3), channel_id=1, source_target_pairs={{0,8},{2,6},{8,16},{10,2},{16,24},{18,10},{24,28},{26,18},{28,20},... | collective-permute-start | bytes 6291464 | tf_op jit(solution)/shard_map/ppermute | solution.py:207
  27.4 37.2 %collective-permute-start = (bf16[2,256,512]{2,1,0:T(8,128)(2,1)S(1)}, bf16[2,256,512]{2,1,0:T(8,128)(2,1)S(1)}, u32[]{:S(2)}, u32[]{:S(2)}) collective-permute-start(bf16[2,256,512]{2,1,0:T(8,128)(2,1)S(1)} %pad_maximum_fusion), channel_id=1, source_target_pairs={{0,4},{2,6},{4,8},{6,10},{8,12},{10,14},{12,16},{14,18},{16,20},{1... | collective-permute-start | bytes 1572872 | tf_op jit(solution)/shard_map/ppermute | solution.py:19
  31.7 32.9 %collective-permute-start.1 = (bf16[2,256,512]{2,1,0:T(8,128)(2,1)S(1)}, bf16[2,256,512]{2,1,0:T(8,128)(2,1)S(1)}, u32[]{:S(2)}, u32[]{:S(2)}) collective-permute-start(bf16[2,256,512]{2,1,0:T(8,128)(2,1)S(1)} %pad_maximum_fusion), channel_id=1, source_target_pairs={{0,2},{2,4},{4,6},{6,8},{8,10},{10,12},{12,14},{14,16},{16,18},{18... | collective-permute-start | bytes 1572872 | tf_op jit(solution)/shard_map/ppermute | solution.py:19
  36.8 67.2 %collective-permute-start.2 = (bf16[256,4096]{1,0:T(8,128)(2,1)}, bf16[256,4096]{1,0:T(8,128)(2,1)}, u32[]{:S(2)}, u32[]{:S(2)}) collective-permute-start(bf16[256,4096]{1,0:T(8,128)(2,1)} %param.12), channel_id=1, source_target_pairs={{0,2},{2,0},{4,6},{6,4},{8,10},{10,8},{12,14},{14,12},{16,18},{18,... | collective-permute-start | bytes 6291464 | tf_op jit(solution)/shard_map/ppermute | solution.py:204
  36.8 57.5 %collective-permute-start.17 = (bf16[256,2048]{1,0:T(8,128)(2,1)}, bf16[256,2048]{1,0:T(8,128)(2,1)S(1)}, u32[]{:S(2)}, u32[]{:S(2)}) collective-permute-start(bf16[256,2048]{1,0:T(8,128)(2,1)} %param.11), channel_id=1, source_target_pairs={{0,1},{1,0},{2,3},{3,2},{4,5},{5,4},{6,7},{7,6},{8,9},{9,8},{10,11... | collective-permute-start | bytes 3145736 | tf_op jit(solution)/shard_map/ppermute | solution.py:23
  66.9 25.8 %copy-start.2 = (bf16[256,4096]{1,0:T(8,128)(2,1)S(1)}, bf16[256,4096]{1,0:T(8,128)(2,1)}, u32[]{:S(2)}) copy-start(bf16[256,4096]{1,0:T(8,128)(2,1)} %param.12) | copy-start | bytes 6291460
  92.4 25.4 %collective-permute-start.7 = (bf16[256,4096]{1,0:T(8,128)(2,1)}, bf16[256,4096]{1,0:T(8,128)(2,1)S(1)}, u32[]{:S(2)}, u32[]{:S(2)}) collective-permute-start(bf16[256,4096]{1,0:T(8,128)(2,1)} %collective-permute-done.5), channel_id=1, source_target_pairs={{0,8},{2,6},{8,16},{10,2},{16,24},{18,10},{24,28},{26,18},{28,20},... | collective-permute-start | bytes 6291464 | tf_op jit(solution)/shard_map/ppermute | solution.py:207
  94.3 1.6 copy-start.3
  97.4 9.7 %copy-start.1 = (bf16[256,4096]{1,0:T(8,128)(2,1)S(1)}, bf16[256,4096]{1,0:T(8,128)(2,1)}, u32[]{:S(2)}) copy-start(bf16[256,4096]{1,0:T(8,128)(2,1)} %get-tuple-element.12.refs_4_) | copy-start | bytes 6291460
  97.4 33.6 %collective-permute-start.4 = (bf16[256,4096]{1,0:T(8,128)(2,1)}, bf16[256,4096]{1,0:T(8,128)(2,1)S(1)}, u32[]{:S(2)}, u32[]{:S(2)}) collective-permute-start(bf16[256,4096]{1,0:T(8,128)(2,1)} %collective-permute-done.3), channel_id=1, source_target_pairs={{0,2},{2,0},{4,6},{6,4},{8,10},{10,8},{12,14},{14,12},{16,18},{18,... | collective-permute-start | bytes 6291464 | tf_op jit(solution)/shard_map/ppermute | solution.py:204
  117.8 25.2 %collective-permute-start.9 = (bf16[256,4096]{1,0:T(8,128)(2,1)S(1)}, bf16[256,4096]{1,0:T(8,128)(2,1)S(1)}, u32[]{:S(2)}, u32[]{:S(2)}) collective-permute-start(bf16[256,4096]{1,0:T(8,128)(2,1)S(1)} %collective-permute-done.7), channel_id=1, source_target_pairs={{0,8},{2,6},{8,16},{10,2},{16,24},{18,10},{24,28},{26,18},{28,20},... | collective-permute-start | bytes 6291464 | tf_op jit(solution)/shard_map/ppermute | solution.py:207
  122.0 22.8 %collective-permute-start.6 = (bf16[256,4096]{1,0:T(8,128)(2,1)}, bf16[256,4096]{1,0:T(8,128)(2,1)S(1)}, u32[]{:S(2)}, u32[]{:S(2)}) collective-permute-start(bf16[256,4096]{1,0:T(8,128)(2,1)} %collective-permute-done.5), channel_id=1, source_target_pairs={{0,2},{2,0},{4,6},{6,4},{8,10},{10,8},{12,14},{14,12},{16,18},{18,... | collective-permute-start | bytes 6291464 | tf_op jit(solution)/shard_map/ppermute | solution.py:204
  133.2 22.9 %collective-permute-start.8 = (bf16[256,4096]{1,0:T(8,128)(2,1)S(1)}, bf16[256,4096]{1,0:T(8,128)(2,1)S(1)}, u32[]{:S(2)}, u32[]{:S(2)}) collective-permute-start(bf16[256,4096]{1,0:T(8,128)(2,1)S(1)} %collective-permute-done.7), channel_id=1, source_target_pairs={{0,2},{2,0},{4,6},{6,4},{8,10},{10,8},{12,14},{14,12},{16,18},{18,... | collective-permute-start | bytes 6291464 | tf_op jit(solution)/shard_map/ppermute | solution.py:204
  143.0 26.4 %collective-permute-start.11 = (bf16[256,4096]{1,0:T(8,128)(2,1)S(1)}, bf16[256,4096]{1,0:T(8,128)(2,1)S(1)}, u32[]{:S(2)}, u32[]{:S(2)}) collective-permute-start(bf16[256,4096]{1,0:T(8,128)(2,1)S(1)} %collective-permute-done.9), channel_id=1, source_target_pairs={{0,8},{2,6},{8,16},{10,2},{16,24},{18,10},{24,28},{26,18},{28,20},... | collective-permute-start | bytes 6291464 | tf_op jit(solution)/shard_map/ppermute | solution.py:207
  147.0 33.7 %collective-permute-start.10 = (bf16[256,4096]{1,0:T(8,128)(2,1)S(1)}, bf16[256,4096]{1,0:T(8,128)(2,1)S(1)}, u32[]{:S(2)}, u32[]{:S(2)}) collective-permute-start(bf16[256,4096]{1,0:T(8,128)(2,1)S(1)} %collective-permute-done.9), channel_id=1, source_target_pairs={{0,2},{2,0},{4,6},{6,4},{8,10},{10,8},{12,14},{14,12},{16,18},{18,... | collective-permute-start | bytes 6291464 | tf_op jit(solution)/shard_map/ppermute | solution.py:204
  169.4 25.2 %collective-permute-start.13 = (bf16[256,4096]{1,0:T(8,128)(2,1)S(1)}, bf16[256,4096]{1,0:T(8,128)(2,1)S(1)}, u32[]{:S(2)}, u32[]{:S(2)}) collective-permute-start(bf16[256,4096]{1,0:T(8,128)(2,1)S(1)} %collective-permute-done.11), channel_id=1, source_target_pairs={{0,8},{2,6},{8,16},{10,2},{16,24},{18,10},{24,28},{26,18},{28,20},... | collective-permute-start | bytes 6291464 | tf_op jit(solution)/shard_map/ppermute | solution.py:207
  172.3 33.7 %collective-permute-start.12 = (bf16[256,4096]{1,0:T(8,128)(2,1)S(1)}, bf16[256,4096]{1,0:T(8,128)(2,1)S(1)}, u32[]{:S(2)}, u32[]{:S(2)}) collective-permute-start(bf16[256,4096]{1,0:T(8,128)(2,1)S(1)} %collective-permute-done.11), channel_id=1, source_target_pairs={{0,2},{2,0},{4,6},{6,4},{8,10},{10,8},{12,14},{14,12},{16,18},{18,... | collective-permute-start | bytes 6291464 | tf_op jit(solution)/shard_map/ppermute | solution.py:204
  194.6 25.2 %collective-permute-start.15 = (bf16[256,4096]{1,0:T(8,128)(2,1)S(1)}, bf16[256,4096]{1,0:T(8,128)(2,1)S(1)}, u32[]{:S(2)}, u32[]{:S(2)}) collective-permute-start(bf16[256,4096]{1,0:T(8,128)(2,1)S(1)} %collective-permute-done.13), channel_id=1, source_target_pairs={{0,8},{2,6},{8,16},{10,2},{16,24},{18,10},{24,28},{26,18},{28,20},... | collective-permute-start | bytes 6291464 | tf_op jit(solution)/shard_map/ppermute | solution.py:207
  196.1 34.0 %collective-permute-start.14 = (bf16[256,4096]{1,0:T(8,128)(2,1)S(1)}, bf16[256,4096]{1,0:T(8,128)(2,1)S(1)}, u32[]{:S(2)}, u32[]{:S(2)}) collective-permute-start(bf16[256,4096]{1,0:T(8,128)(2,1)S(1)} %collective-permute-done.13), channel_id=1, source_target_pairs={{0,2},{2,0},{4,6},{6,4},{8,10},{10,8},{12,14},{14,12},{16,18},{18,... | collective-permute-start | bytes 6291464 | tf_op jit(solution)/shard_map/ppermute | solution.py:204
  219.8 14.0 %collective-permute-start.16 = (bf16[256,4096]{1,0:T(8,128)(2,1)S(1)}, bf16[256,4096]{1,0:T(8,128)(2,1)S(1)}, u32[]{:S(2)}, u32[]{:S(2)}) collective-permute-start(bf16[256,4096]{1,0:T(8,128)(2,1)S(1)} %collective-permute-done.15), channel_id=1, source_target_pairs={{0,2},{2,0},{4,6},{6,4},{8,10},{10,8},{12,14},{14,12},{16,18},{18,... | collective-permute-start | bytes 6291464 | tf_op jit(solution)/shard_map/ppermute | solution.py:204
  234.5 1.9 copy-start
  260.3 14.9 %collective-permute-start.19 = (bf16[2,256,512]{2,1,0:T(8,128)(2,1)}, bf16[2,256,512]{2,1,0:T(8,128)(2,1)S(1)}, u32[]{:S(2)}, u32[]{:S(2)}) collective-permute-start(bf16[2,256,512]{2,1,0:T(8,128)(2,1)} %get-tuple-element.18), channel_id=1, source_target_pairs={{2,0},{4,2},{6,4},{8,6},{10,8},{12,10},{14,12},{16,14},{18,16},{20... | collective-permute-start | bytes 1572872 | tf_op jit(solution)/shard_map/ppermute | solution.py:19
  262.3 16.4 %collective-permute-start.20 = (bf16[2,256,512]{2,1,0:T(8,128)(2,1)}, bf16[2,256,512]{2,1,0:T(8,128)(2,1)S(1)}, u32[]{:S(2)}, u32[]{:S(2)}) collective-permute-start(bf16[2,256,512]{2,1,0:T(8,128)(2,1)} %get-tuple-element.19), channel_id=1, source_target_pairs={{4,0},{6,2},{8,4},{10,6},{12,8},{14,10},{16,12},{18,14},{20,16},{2... | collective-permute-start | bytes 1572872 | tf_op jit(solution)/shard_map/ppermute | solution.py:19
  265.4 24.0 %collective-permute-start.18 = (bf16[256,2048]{1,0:T(8,128)(2,1)S(1)}, bf16[256,2048]{1,0:T(8,128)(2,1)S(1)}, u32[]{:S(2)}, u32[]{:S(2)}) collective-permute-start(bf16[256,2048]{1,0:T(8,128)(2,1)S(1)} %dynamic-slice_convert_fusion), channel_id=1, source_target_pairs={{0,1},{1,0},{2,3},{3,2},{4,5},{5,4},{6,7},{7,6},{8,9},{9,8},{10,11... | collective-permute-start | bytes 3145736 | tf_op jit(solution)/shard_map/ppermute | solution.py:23
